TPU v7x, 32 devices: a whole 2x2x4 slice. The times are simulated.
32 devices in a mesh: pole: 2 (over y), row: 4 (over x, core), col: 4 (over z).
Axes of the slice: x: 2, y: 2, z: 4, core: 2. Of those that a mesh axis runs over, the one named last changes fastest.
Arguments:
- inverse_blocks: float32 [4096, 2048], P(('pole', 'row'), 'col'), parts along dimension 0, may hold values from -6 to 6
- lower_panel: float32 [4096, 512], P(('pole', 'row'), 'col'), parts along dimension 0, may hold values from -0.125 to 0.125
- struct_mask: int32 [16, 4], P('row', 'col'), may hold values 0 or 1
- diag_inverse: float32 [1024, 128], P(('pole', 'col')), parts along dimension 0, may hold values from -6 to 6
Outputs:
- g_panel: float32 [4096, 512], P(('pole', 'row'), 'col'), parts along dimension 0
- g_diag: float32 [1024, 128], P(('pole', 'col')), parts along dimension 0
There are 2 independent parts, one for each index of `pole`. A program takes and returns all parts, laid end to end along the dimension named above; an argument that names none is the same for every part. Nothing has to cross between parts.
All inputs are finite; a program needn't handle non-finite values. No bound on the sum of `struct_mask` on one device may be relied on, other than what follows from the above.
Results may differ from a plain program's by a relative error of at most 0.000071.
Values sent between devices are 32-bit elements; how exact they have to be, the bound alone decides.
No kernel may reach another device: no remote copies, remote signals or barrier semaphores. Data moves between devices by JAX's collectives and lax.ppermute only.
A program may use at most 64 MiB of HBM per device.

v0:
```python
import jax
import jax.numpy as jnp
from jax import lax
from jax.sharding import PartitionSpec as P


def from_root(x, axis, root):
    mine = lax.axis_index(axis) == root
    return lax.psum(jnp.where(mine, x, jnp.zeros_like(x)), axis)


def on_device(inverse_blocks, lower_panel, struct_mask, diag_inverse):
    width = diag_inverse.shape[1]
    local_rows = lower_panel.shape[0]
    local_cols = lower_panel.shape[1]
    supers = local_cols // width
    expanded = jnp.repeat(jnp.repeat(struct_mask, width, axis=0), width, axis=1).astype(jnp.float32)
    masked = lower_panel * expanded
    panel_row = lax.all_gather(masked, "col", axis=1, tiled=True)
    mirrored = from_root(panel_row, "row", lax.axis_index("col"))
    summed = lax.psum_scatter(
        lax.dot_general(
            mirrored,
            inverse_blocks,
            (((0,), (1,)), ((), ())),
            precision=lax.Precision.HIGHEST,
            preferred_element_type=jnp.float32,
        ),
        "col",
        scatter_dimension=0,
        tiled=True,
    )
    g_panel = -summed.T * expanded
    masked_three = masked.reshape(local_rows, supers, width)
    panel_three = g_panel.reshape(local_rows, supers, width)
    quad_part = -jnp.einsum(
        "jka,jkb->kab", masked_three, panel_three, precision=lax.Precision.HIGHEST
    )
    quad_total = lax.psum(quad_part, "row")
    g_diag = diag_inverse + quad_total.reshape(supers * width, width)
    return (g_panel, g_diag)


def solution(mesh):
    placed = (
        P(("pole", "row"), "col"),
        P(("pole", "row"), "col"),
        P("row", "col"),
        P(("pole", "col"), None),
    )
    return jax.shard_map(
        on_device,
        mesh=mesh,
        in_specs=placed,
        out_specs=(P(("pole", "row"), "col"), P(("pole", "col"), None)),
        check_vma=False,
    )
```

profile of v0, /device:TPU:0, one launch (start us, length us, event | category | flops | bytes accessed | tf_op | source)
XLA Modules:
  0.0 153.8 jit_solution(16746672606810595600)
XLA Ops:
  7.2 0.0 copy-start
  7.2 0.0 all-gather.2.cloned.1.call-start
  7.2 0.7 convert_bitcast_fusion
  8.0 0.1 broadcast_bitcast_fusion
  8.0 1.8 %broadcast_multiply_fusion = f32[512,128]{1,0:T(8,128)} fusion(f32[512,128]{1,0:T(8,128)} %param.5, f32[512]{0:T(512)S(1)} %broadcast_bitcast_fusion), kind=kLoop, calls=%fused_computation.5 | loop fusion | flops 65536 | bytes 526336 | tf_op jit(solution)/shard_map/mul | solution.py:18
  9.8 0.0 all-gather.2.cloned.1.call-update
  9.8 0.0 all-reduce.3.cloned.1.call-start
  9.9 33.2 %all-gather.2.cloned.1.call-done = f32[512,512]{1,0:T(8,128)} async-done(((f32[512,128]{1,0:T(8,128)}), f32[512,512]{1,0:T(8,128)}) %all-gather.2.cloned.1.call-update) | async-done | bytes 1048592 | tf_op jit(solution)/shard_map/all_gather | solution.py:19
  43.1 2.3 %broadcast_select_fusion = f32[512,512]{1,0:T(8,128)} fusion(f32[512,512]{1,0:T(8,128)} %all-gather.2.cloned.1.call-done, pred[]{:T(512)S(6)} %eq.3), kind=kLoop, calls=%fused_computation.1 | loop fusion | flops 262144 | bytes 2097153 | tf_op jit(solution)/shard_map/jit(_where)/select_n | solution.py:9
  45.4 0.0 all-reduce.3.cloned.1.call-update
  45.4 0.0 reduce-scatter.2.cloned.1.call-start
  45.5 34.4 %all-reduce.3.cloned.1.call-done = f32[512,512]{1,0:T(8,128)} async-done(((f32[512,512]{1,0:T(8,128)}), f32[512,512]{1,0:T(8,128)}) %all-reduce.3.cloned.1.call-update) | async-done | bytes 1048592 | tf_op jit(solution)/shard_map/psum | solution.py:9
  79.9 0.0 copy-done
  79.9 5.7 %fusion.2 = f32[512,512]{1,0:T(8,128)} fusion(f32[512,512]{1,0:T(8,128)} %all-reduce.3.cloned.1.call-done, f32[512,512]{1,0:T(8,128)S(1)} %copy-done), kind=kOutput, calls=%fused_computation.8 | convolution fusion | flops 1610612736 | bytes 3145728 | tf_op jit(solution)/shard_map/dot_general | solution.py:22
  85.6 0.0 copy-start.1
  85.6 0.0 reduce-scatter.2.cloned.1.call-update
  85.7 0.0 all-reduce.5.cloned.1.call-start
  85.7 27.6 %reduce-scatter.2.cloned.1.call-done = f32[128,512]{1,0:T(8,128)} async-done(((f32[512,512]{1,0:T(8,128)}), f32[128,512]{1,0:T(8,128)}) %reduce-scatter.2.cloned.1.call-update) | async-done | bytes 262160 | tf_op jit(solution)/shard_map/reduce_scatter | solution.py:21
  113.3 0.0 copy-done.1
  113.4 0.0 copy-start.2
  113.4 2.3 %convolution_negate_fusion = f32[128,128]{1,0:T(8,128)} fusion(f32[128,512]{1,0:T(8,128)} %reduce-scatter.2.cloned.1.call-done, f32[512]{0:T(512)S(1)} %broadcast_bitcast_fusion, f32[512,128]{1,0:T(8,128)S(1)} %copy-done.1), kind=kOutput, calls=%fused_computation | convolution fusion | flops 100876288 | bytes 591872 | tf_op jit(solution)/shard_map/jka,jkb->kab/dot_general | solution.py:36
  115.7 0.0 all-reduce.5.cloned.1.call-update
  115.7 0.0 copy-done.2
  115.8 0.0 copy-start.3
  115.8 0.8 copy.6
  116.6 29.2 %all-reduce.5.cloned.1.call-done = f32[128,128]{1,0:T(8,128)} async-done(((f32[128,128]{1,0:T(8,128)}), f32[128,128]{1,0:T(8,128)}) %all-reduce.5.cloned.1.call-update) | async-done | bytes 65552 | tf_op jit(solution)/shard_map/psum | solution.py:39
  145.8 0.0 copy-done.3
  145.8 1.5 add.9
  (1 shorter events, 0.0 us)
Async XLA Ops:
  7.2 72.7 %copy-start = (f32[512,512]{1,0:T(8,128)S(1)}, f32[512,512]{1,0:T(8,128)}, u32[]{:S(2)}) copy-start(f32[512,512]{1,0:T(8,128)} %param.4) | copy-start | bytes 3145732
  7.2 35.9 %all-gather.2.cloned.1.call-start = ((), (), s32[]{:S(2)}) async-start(), calls=%async_computation.1 | async-start | bytes 1310720 | tf_op jit(solution)/shard_map/all_gather | solution.py:19
  9.8 70.1 %all-reduce.3.cloned.1.call-start = ((), (), s32[]{:S(2)}) async-start(), calls=%async_computation.2 | async-start | bytes 2097152 | tf_op jit(solution)/shard_map/psum | solution.py:9
  45.4 67.9 %reduce-scatter.2.cloned.1.call-start = ((), (), s32[]{:S(2)}) async-start(), calls=%async_computation.3 | async-start | bytes 1310720 | tf_op jit(solution)/shard_map/reduce_scatter | solution.py:21
  85.6 27.7 %copy-start.1 = (f32[512,128]{1,0:T(8,128)S(1)}, f32[512,128]{1,0:T(8,128)}, u32[]{:S(2)}) copy-start(f32[512,128]{1,0:T(8,128)} %param.5) | copy-start | bytes 786436
  85.7 60.2 %all-reduce.5.cloned.1.call-start = ((), (), s32[]{:S(2)}) async-start(), calls=%async_computation.4 | async-start | bytes 131072 | tf_op jit(solution)/shard_map/psum | solution.py:39
  113.4 2.4 %copy-start.2 = (f32[128,512]{1,0:T(8,128)S(1)}, f32[128,512]{1,0:T(8,128)}, u32[]{:S(2)}) copy-start(f32[128,512]{1,0:T(8,128)} %reduce-scatter.2.cloned.1.call-done) | copy-start | bytes 786436
  115.8 30.1 %copy-start.3 = (f32[128,128]{1,0:T(8,128)S(1)}, f32[128,128]{1,0:T(8,128)}, u32[]{:S(2)}) copy-start(f32[128,128]{1,0:T(8,128)} %param.7) | copy-start | bytes 196612
Sparse Core Ops, SparseCore 0:
  10.1 32.8 all-gather.1
  45.6 34.2 all-reduce.2
  85.8 27.5 reduce-scatter.1
  116.1 29.6 all-reduce.4
where the time goes:
time: 154 us
  waiting for transfers between devices  124 us (81%)
  between operations  13.8 us (9%)
  matrix products  8.07 us (5%)
  other arithmetic  6.37 us (4%)
    psum x1, waiting for transfers between devices, from_root(): return lax.psum(jnp.where(mine, x, jnp.zeros_like(x)), axis)  34.4 us
    all_gather x1, waiting for transfers between devices, on_device(): panel_row = lax.all_gather(masked, 'col', axis=1, tiled=True)  33.2 us
    psum x1, waiting for transfers between devices, on_device(): quad_total = lax.psum(quad_part, 'row')  29.2 us
    reduce_scatter x1, waiting for transfers between devices, on_device(): lax.psum_scatter(lax.dot_general(mirrored, inverse_blocks, (((0,), (1,)),...  27.6 us
    dot_general x1, matrix products, on_device(): lax.dot_general(mirrored, inverse_blocks, (((0,), (1,)), ((), ())), preci...  5.73 us
  transfers between devices with their start and end apart: 4, of which 4 were waited for; matrix products, arithmetic and copies ran while one was open for 1% of the time, Pallas kernels for 0%

commit v1 on v0

--- a/solution.py
+++ b/solution.py
@@ -2,6 +2,16 @@
 import jax.numpy as jnp
 from jax import lax
 from jax.sharding import PartitionSpec as P
+
+
+def collect(x, axis, dim):
+    ways, here, lap = (lax.axis_size(axis), lax.axis_index(axis), x.shape[dim])
+    shape = [n * ways if d == dim else n for d, n in enumerate(x.shape)]
+    full = lax.dynamic_update_slice_in_dim(jnp.zeros(shape, x.dtype), x, here * lap, axis=dim)
+    for far in range(1, ways):
+        x = lax.ppermute(x, axis, [(d, (d + 1) % ways) for d in range(ways)])
+        full = lax.dynamic_update_slice_in_dim(full, x, (here - far) % ways * lap, axis=dim)
+    return full
 
 
 def from_root(x, axis, root):
@@ -16,7 +26,7 @@
     supers = local_cols // width
     expanded = jnp.repeat(jnp.repeat(struct_mask, width, axis=0), width, axis=1).astype(jnp.float32)
     masked = lower_panel * expanded
-    panel_row = lax.all_gather(masked, "col", axis=1, tiled=True)
+    panel_row = collect(masked, "col", 1)
     mirrored = from_root(panel_row, "row", lax.axis_index("col"))
     summed = lax.psum_scatter(
         lax.dot_general(

time: 154 us -> 148 us (0.961)
  waiting for transfers between devices: 124 us -> 117 us
  other arithmetic: 6.37 us -> 2.75 us
  starting transfers between devices: 0.16 us -> 3.2 us
  local copies, waits for them, and re-layouts: 0.93 us -> 2.68 us
    all_gather x1 -> x0, waiting for transfers between devices: 33.2 us -> none  [on_device(): panel_row = lax.all_gather(masked, 'col', axis=1, tiled=True)]
    ppermute x0 -> x3, waiting for transfers between devices: none -> 25.9 us  [collect(): x = lax.ppermute(x, axis, [(d, (d + 1) % ways) for d in range(ways)])]
    ppermute x0 -> x3, starting transfers between devices: none -> 3.08 us  [collect(): x = lax.ppermute(x, axis, [(d, (d + 1) % ways) for d in range(ways)])]
    mul x1 -> x0, other arithmetic: 1.79 us -> none  [on_device(): masked = lower_panel * expanded]
    unnamed x9 -> x11, local copies, waits for them, and re-layouts: 0.86 us -> 2.41 us
  transfers between devices with their start and end apart: 4 -> 6, of which waited for: 4 -> 6; matrix products, arithmetic and copies ran while one was open for 1% -> 1% of each run, Pallas kernels for 0% -> 0%
where the time goes in v1:
time: 148 us; the launch traced here: 147 us
  waiting for transfers between devices  117 us (79%)
  between operations  13.8 us (9%)
  matrix products  7.96 us (5%)
  starting transfers between devices  3.2 us (2%)
  other arithmetic  2.75 us (2%)
  local copies, waits for them, and re-layouts  2.68 us (2%)
    psum x1, waiting for transfers between devices, from_root(): return lax.psum(jnp.where(mine, x, jnp.zeros_like(x)), axis)  34 us
    psum x1, waiting for transfers between devices, on_device(): quad_total = lax.psum(quad_part, 'row')  29.5 us
    reduce_scatter x1, waiting for transfers between devices, on_device(): lax.psum_scatter(lax.dot_general(mirrored, inverse_blocks, (((0,), (1,)),...  27.6 us
    ppermute x3, waiting for transfers between devices, collect(): x = lax.ppermute(x, axis, [(d, (d + 1) % ways) for d in range(ways)])  25.9 us
    dot_general x1, matrix products, on_device(): lax.dot_general(mirrored, inverse_blocks, (((0,), (1,)), ((), ())), preci...  5.72 us
    ppermute x3, starting transfers between devices, collect(): x = lax.ppermute(x, axis, [(d, (d + 1) % ways) for d in range(ways)])  3.08 us
  transfers between devices with their start and end apart: 6, of which 6 were waited for; matrix products, arithmetic and copies ran while one was open for 1% of the time, Pallas kernels for 0%

profile of v1, /device:TPU:0, one launch (start us, length us, event | category | flops | bytes accessed | tf_op | source)
XLA Modules:
  0.0 147.5 jit_solution(8218560939800806073)
XLA Ops:
  7.2 0.0 copy-start
  7.2 0.0 all-reduce.3.cloned.1.call-start
  7.2 0.0 copy-start.4
  7.2 0.7 copy-done.4
  8.0 0.1 broadcast_bitcast_fusion
  8.0 0.0 copy-start.2
  8.0 0.1 broadcast.14
  8.2 0.8 copy-done.2
  9.0 0.1 constant_dynamic-update-slice_fusion.3
  9.1 3.1 %collective-permute-start = (f32[512,128]{1,0:T(8,128)S(1)}, f32[512,128]{1,0:T(8,128)S(1)}, u32[]{:S(2)}, u32[]{:S(2)}) collective-permute-start(f32[512,128]{1,0:T(8,128)S(1)} %get-tuple-element.5), channel_id=1, source_target_pairs={{0,1},{1,2},{2,3},{3,0},{4,5},{5,6},{6,7},{7,4},{8,9},{9,10},{10,1... | collective-permute-start | bytes 786440 | tf_op jit(solution)/shard_map/ppermute | solution.py:12
  12.2 8.3 %collective-permute-done = f32[512,128]{1,0:T(8,128)S(1)} collective-permute-done((f32[512,128]{1,0:T(8,128)S(1)}, f32[512,128]{1,0:T(8,128)S(1)}, u32[]{:S(2)}, u32[]{:S(2)}) %collective-permute-start) | collective-permute-done | bytes 262176 | tf_op jit(solution)/shard_map/ppermute | solution.py:12
  20.5 0.0 collective-permute-start.1
  20.5 9.3 %collective-permute-done.1 = f32[512,128]{1,0:T(8,128)S(1)} collective-permute-done((f32[512,128]{1,0:T(8,128)S(1)}, f32[512,128]{1,0:T(8,128)S(1)}, u32[]{:S(2)}, u32[]{:S(2)}) %collective-permute-start.1) | collective-permute-done | bytes 262176 | tf_op jit(solution)/shard_map/ppermute | solution.py:12
  29.8 0.0 collective-permute-start.2
  29.9 8.3 %collective-permute-done.2 = f32[512,128]{1,0:T(8,128)S(1)} collective-permute-done((f32[512,128]{1,0:T(8,128)S(1)}, f32[512,128]{1,0:T(8,128)S(1)}, u32[]{:S(2)}, u32[]{:S(2)}) %collective-permute-start.2) | collective-permute-done | bytes 262176 | tf_op jit(solution)/shard_map/ppermute | solution.py:12
  38.2 1.1 broadcast_select_fusion
  39.3 0.0 all-reduce.3.cloned.1.call-update
  39.4 0.0 reduce-scatter.2.cloned.1.call-start
  39.4 34.0 %all-reduce.3.cloned.1.call-done = f32[512,512]{1,0:T(8,128)} async-done(((f32[512,512]{1,0:T(8,128)}), f32[512,512]{1,0:T(8,128)}) %all-reduce.3.cloned.1.call-update) | async-done | bytes 1048592 | tf_op jit(solution)/shard_map/psum | solution.py:19
  73.4 0.0 copy-done
  73.4 5.7 %fusion.2 = f32[512,512]{1,0:T(8,128)} fusion(f32[512,512]{1,0:T(8,128)} %all-reduce.3.cloned.1.call-done, f32[512,512]{1,0:T(8,128)S(1)} %copy-done), kind=kOutput, calls=%fused_computation.12 | convolution fusion | flops 1610612736 | bytes 3145728 | tf_op jit(solution)/shard_map/dot_general | solution.py:32
  79.1 0.0 reduce-scatter.2.cloned.1.call-update
  79.1 0.0 all-reduce.5.cloned.1.call-start
  79.2 27.6 %reduce-scatter.2.cloned.1.call-done = f32[128,512]{1,0:T(8,128)} async-done(((f32[512,512]{1,0:T(8,128)}), f32[128,512]{1,0:T(8,128)}) %reduce-scatter.2.cloned.1.call-update) | async-done | bytes 262160 | tf_op jit(solution)/shard_map/reduce_scatter | solution.py:31
  106.8 2.2 %convolution_negate_fusion = f32[128,128]{1,0:T(8,128)} fusion(f32[512,128]{1,0:T(8,128)S(1)} %get-tuple-element.5, f32[128,512]{1,0:T(8,128)} %reduce-scatter.2.cloned.1.call-done, f32[512]{0:T(512)S(1)} %broadcast_bitcast_fusion), kind=kOutput, calls=%fused_computation | convolution fusion | flops 100810752 | bytes 591872 | tf_op jit(solution)/shard_map/jka,jkb->kab/dot_general | solution.py:46
  109.1 0.0 all-reduce.5.cloned.1.call-update
  109.1 0.0 copy-done.1
  109.1 0.0 copy-start.3
  109.2 0.8 copy.6
  110.0 29.5 %all-reduce.5.cloned.1.call-done = f32[128,128]{1,0:T(8,128)} async-done(((f32[128,128]{1,0:T(8,128)}), f32[128,128]{1,0:T(8,128)}) %all-reduce.5.cloned.1.call-update) | async-done | bytes 65552 | tf_op jit(solution)/shard_map/psum | solution.py:49
  139.5 0.0 copy-done.3
  139.5 1.5 %add.41 = f32[128,128]{1,0:T(8,128)} add(f32[128,128]{1,0:T(8,128)S(1)} %copy-done.3, f32[128,128]{1,0:T(8,128)} %all-reduce.5.cloned.1.call-done) | non-fusion elementwise | flops 16384 | bytes 196608 | tf_op jit(solution)/shard_map/add | solution.py:50
  (6 shorter events, 0.1 us)
Async XLA Ops:
  7.2 66.2 %copy-start = (f32[512,512]{1,0:T(8,128)S(1)}, f32[512,512]{1,0:T(8,128)}, u32[]{:S(2)}) copy-start(f32[512,512]{1,0:T(8,128)} %param.4) | copy-start | bytes 3145732
  7.2 66.2 %all-reduce.3.cloned.1.call-start = ((), (), s32[]{:S(2)}) async-start(), calls=%async_computation.1 | async-start | bytes 2097152 | tf_op jit(solution)/shard_map/psum | solution.py:19
  7.2 0.7 copy-start.4
  8.0 0.9 copy-start.2
  9.1 11.4 %collective-permute-start = (f32[512,128]{1,0:T(8,128)S(1)}, f32[512,128]{1,0:T(8,128)S(1)}, u32[]{:S(2)}, u32[]{:S(2)}) collective-permute-start(f32[512,128]{1,0:T(8,128)S(1)} %get-tuple-element.5), channel_id=1, source_target_pairs={{0,1},{1,2},{2,3},{3,0},{4,5},{5,6},{6,7},{7,4},{8,9},{9,10},{10,1... | collective-permute-start | bytes 786440 | tf_op jit(solution)/shard_map/ppermute | solution.py:12
  20.5 9.3 %collective-permute-start.1 = (f32[512,128]{1,0:T(8,128)S(1)}, f32[512,128]{1,0:T(8,128)S(1)}, u32[]{:S(2)}, u32[]{:S(2)}) collective-permute-start(f32[512,128]{1,0:T(8,128)S(1)} %collective-permute-done), channel_id=1, source_target_pairs={{0,1},{1,2},{2,3},{3,0},{4,5},{5,6},{6,7},{7,4},{8,9},{9,10},{10,1... | collective-permute-start | bytes 786440 | tf_op jit(solution)/shard_map/ppermute | solution.py:12
  29.8 8.4 %collective-permute-start.2 = (f32[512,128]{1,0:T(8,128)S(1)}, f32[512,128]{1,0:T(8,128)S(1)}, u32[]{:S(2)}, u32[]{:S(2)}) collective-permute-start(f32[512,128]{1,0:T(8,128)S(1)} %collective-permute-done.1), channel_id=1, source_target_pairs={{0,1},{1,2},{2,3},{3,0},{4,5},{5,6},{6,7},{7,4},{8,9},{9,10},{10,1... | collective-permute-start | bytes 786440 | tf_op jit(solution)/shard_map/ppermute | solution.py:12
  39.4 67.5 %reduce-scatter.2.cloned.1.call-start = ((), (), s32[]{:S(2)}) async-start(), calls=%async_computation.2 | async-start | bytes 1310720 | tf_op jit(solution)/shard_map/reduce_scatter | solution.py:31
  79.1 60.3 %all-reduce.5.cloned.1.call-start = ((), (), s32[]{:S(2)}) async-start(), calls=%async_computation.3 | async-start | bytes 131072 | tf_op jit(solution)/shard_map/psum | solution.py:49
  106.8 2.3 %copy-start.1 = (f32[128,512]{1,0:T(8,128)S(1)}, f32[128,512]{1,0:T(8,128)}, u32[]{:S(2)}) copy-start(f32[128,512]{1,0:T(8,128)} %reduce-scatter.2.cloned.1.call-done) | copy-start | bytes 786436
  109.1 30.3 %copy-start.3 = (f32[128,128]{1,0:T(8,128)S(1)}, f32[128,128]{1,0:T(8,128)}, u32[]{:S(2)}) copy-start(f32[128,128]{1,0:T(8,128)} %param.7) | copy-start | bytes 196612
Sparse Core Ops, SparseCore 0:
  39.5 33.8 all-reduce.2
  79.3 27.5 reduce-scatter.1
  109.7 29.6 all-reduce.4

commit v2 on v0

--- a/solution.py
+++ b/solution.py
@@ -36,7 +36,7 @@
     quad_part = -jnp.einsum(
         "jka,jkb->kab", masked_three, panel_three, precision=lax.Precision.HIGHEST
     )
-    quad_total = lax.psum(quad_part, "row")
+    quad_total = jnp.sum(lax.all_gather(quad_part, "row"), axis=0)
     g_diag = diag_inverse + quad_total.reshape(supers * width, width)
     return (g_panel, g_diag)
 

time: 154 us -> 130 us (0.84)
  waiting for transfers between devices: 124 us -> 95.3 us
  blocking collectives: 0 us -> 5.79 us
  matrix products: 8.07 us -> 6.39 us
    psum x1 -> x0, waiting for transfers between devices: 29.2 us -> none  [on_device(): quad_total = lax.psum(quad_part, 'row')]
    all_gather x0 -> x1, blocking collectives: none -> 5.79 us  [on_device(): quad_total = jnp.sum(lax.all_gather(quad_part, 'row'), axis=0)]
    dot_general x1, matrix products: 2.34 us -> 0.69 us  [on_device(): jnp.einsum('jka,jkb->kab', masked_three, panel_three, precision=lax.Preci...]
  transfers between devices with their start and end apart: 4 -> 3, of which waited for: 4 -> 3; matrix products, arithmetic and copies ran while one was open for 1% -> 0% of each run, Pallas kernels for 0% -> 0%
where the time goes in v2:
time: 130 us
  waiting for transfers between devices  95.3 us (73%)
  between operations  13.8 us (11%)
  other arithmetic  6.47 us (5%)
  matrix products  6.39 us (5%)
  blocking collectives  5.79 us (4%)
  local copies, waits for them, and re-layouts  1.92 us (1%)
    psum x1, waiting for transfers between devices, from_root(): return lax.psum(jnp.where(mine, x, jnp.zeros_like(x)), axis)  34.4 us
    all_gather x1, waiting for transfers between devices, on_device(): panel_row = lax.all_gather(masked, 'col', axis=1, tiled=True)  33.2 us
    reduce_scatter x1, waiting for transfers between devices, on_device(): lax.psum_scatter(lax.dot_general(mirrored, inverse_blocks, (((0,), (1,)),...  27.7 us
    all_gather x1, blocking collectives, on_device(): quad_total = jnp.sum(lax.all_gather(quad_part, 'row'), axis=0)  5.79 us
    dot_general x1, matrix products, on_device(): lax.dot_general(mirrored, inverse_blocks, (((0,), (1,)), ((), ())), preci...  5.71 us
  transfers between devices with their start and end apart: 3, of which 3 were waited for; matrix products, arithmetic and copies ran while one was open for 0% of the time, Pallas kernels for 0%

profile of v2, /device:TPU:0, one launch (start us, length us, event | category | flops | bytes accessed | tf_op | source)
XLA Modules:
  0.0 129.8 jit_solution(16104490052188918264)
XLA Ops:
  7.2 0.0 copy-start
  7.2 0.0 all-gather.3.cloned.1.call-start
  7.2 0.7 convert_bitcast_fusion
  8.0 0.1 broadcast_bitcast_fusion
  8.0 1.8 %broadcast_multiply_fusion = f32[512,128]{1,0:T(8,128)} fusion(f32[512,128]{1,0:T(8,128)} %param.5, f32[512]{0:T(512)S(1)} %broadcast_bitcast_fusion), kind=kLoop, calls=%fused_computation.5 | loop fusion | flops 65536 | bytes 526336 | tf_op jit(solution)/shard_map/mul | solution.py:18
  9.8 0.0 all-gather.3.cloned.1.call-update
  9.8 0.0 all-reduce.2.cloned.1.call-start
  9.9 33.2 %all-gather.3.cloned.1.call-done = f32[512,512]{1,0:T(8,128)} async-done(((f32[512,128]{1,0:T(8,128)}), f32[512,512]{1,0:T(8,128)}) %all-gather.3.cloned.1.call-update) | async-done | bytes 1048592 | tf_op jit(solution)/shard_map/all_gather | solution.py:19
  43.1 2.3 %broadcast_select_fusion = f32[512,512]{1,0:T(8,128)} fusion(f32[512,512]{1,0:T(8,128)} %all-gather.3.cloned.1.call-done, pred[]{:T(512)S(6)} %eq.3), kind=kLoop, calls=%fused_computation.1 | loop fusion | flops 262144 | bytes 2097153 | tf_op jit(solution)/shard_map/jit(_where)/select_n | solution.py:9
  45.4 0.0 all-reduce.2.cloned.1.call-update
  45.4 0.0 reduce-scatter.2.cloned.1.call-start
  45.5 34.4 %all-reduce.2.cloned.1.call-done = f32[512,512]{1,0:T(8,128)} async-done(((f32[512,512]{1,0:T(8,128)}), f32[512,512]{1,0:T(8,128)}) %all-reduce.2.cloned.1.call-update) | async-done | bytes 1048592 | tf_op jit(solution)/shard_map/psum | solution.py:9
  79.8 0.0 copy-done
  79.9 5.7 %fusion.2 = f32[512,512]{1,0:T(8,128)} fusion(f32[512,512]{1,0:T(8,128)} %all-reduce.2.cloned.1.call-done, f32[512,512]{1,0:T(8,128)S(1)} %copy-done), kind=kOutput, calls=%fused_computation.8 | convolution fusion | flops 1610612736 | bytes 3145728 | tf_op jit(solution)/shard_map/dot_general | solution.py:22
  85.6 0.0 reduce-scatter.2.cloned.1.call-update
  85.6 27.7 %reduce-scatter.2.cloned.1.call-done = f32[128,512]{1,0:T(8,128)} async-done(((f32[512,512]{1,0:T(8,128)}), f32[128,512]{1,0:T(8,128)}) %reduce-scatter.2.cloned.1.call-update) | async-done | bytes 262160 | tf_op jit(solution)/shard_map/reduce_scatter | solution.py:21
  113.3 1.0 fusion
  114.2 0.0 copy-start.1
  114.3 0.0 copy-start.2
  114.3 0.8 copy.6
  115.1 0.1 copy-done.1
  115.2 0.1 copy-done.2
  115.3 0.7 convolution_negate_fusion
  116.0 5.8 %all-gather = f32[512,128]{1,0:T(8,128)S(1)} all-gather(f32[128,128]{1,0:T(8,128)S(1)} %convolution_negate_fusion), channel_id=2, replica_groups=mesh['pole'=2,'row'=4,'col'=4] {'row'}, dimensions={0}, use_global_device_ids=true | all-gather | bytes 327680 | tf_op jit(solution)/shard_map/all_gather | solution.py:39
  121.8 0.0 copy-start.3
  121.8 0.8 copy-done.3
  122.6 0.6 add.7
  (1 shorter events, 0.0 us)
Async XLA Ops:
  7.2 72.7 %copy-start = (f32[512,512]{1,0:T(8,128)S(1)}, f32[512,512]{1,0:T(8,128)}, u32[]{:S(2)}) copy-start(f32[512,512]{1,0:T(8,128)} %param.4) | copy-start | bytes 3145732
  7.2 35.9 %all-gather.3.cloned.1.call-start = ((), (), s32[]{:S(2)}) async-start(), calls=%async_computation.1 | async-start | bytes 1310720 | tf_op jit(solution)/shard_map/all_gather | solution.py:19
  9.8 70.0 %all-reduce.2.cloned.1.call-start = ((), (), s32[]{:S(2)}) async-start(), calls=%async_computation.2 | async-start | bytes 2097152 | tf_op jit(solution)/shard_map/psum | solution.py:9
  45.4 67.8 %reduce-scatter.2.cloned.1.call-start = ((), (), s32[]{:S(2)}) async-start(), calls=%async_computation.3 | async-start | bytes 1310720 | tf_op jit(solution)/shard_map/reduce_scatter | solution.py:21
  114.2 1.0 copy-start.1
  114.3 1.0 copy-start.2
  121.8 0.8 copy-start.3
Sparse Core Ops, SparseCore 0:
  10.1 32.8 all-gather.2
  45.5 34.2 all-reduce.1
  85.7 27.5 reduce-scatter.1
